TPU v7x, 32 devices: a whole 2x2x4 slice. The times are simulated.
32 devices in a mesh: fsdp: 8 (over z, core), seq: 4 (over y, x).
Axes of the slice: x: 2, y: 2, z: 4, core: 2. Of those that a mesh axis runs over, the one named last changes fastest.
Arguments:
- inputs: bfloat16 [8, 1024, 2048], P('fsdp', 'seq'), may hold values from -6 to 6
- cotangent: bfloat16 [8, 1024, 2048], P('fsdp', 'seq'), may hold values from -6 to 6
- norm1_gain: bfloat16 [2048], P('fsdp'), may hold values from 0.5 to 1.5
- w_qkv: bfloat16 [2048, 6144], P('fsdp'), may hold values from -0.125 to 0.125
- w_beta: bfloat16 [2048, 16], P('fsdp'), may hold values from -0.125 to 0.125
- conv_weight: bfloat16 [2048, 12], P('fsdp'), may hold values from -3 to 3
- out_gain: bfloat16 [128], replicated, may hold values from 0.5 to 1.5
- w_out: bfloat16 [2048, 2048], P('fsdp'), may hold values from -0.125 to 0.125
- norm2_gain: bfloat16 [2048], P('fsdp'), may hold values from 0.5 to 1.5
- w_gate_up: bfloat16 [2048, 11264], P('fsdp'), may hold values from -0.125 to 0.125
- w_down: bfloat16 [5632, 2048], P('fsdp'), may hold values from -0.15625 to 0.15625
Outputs:
- output: bfloat16 [8, 1024, 2048], P('fsdp', 'seq')
- grad_input: float32 [8, 1024, 2048], P('fsdp', 'seq')
- grad_norm1_gain: float32 [2048], P('fsdp')
- grad_w_qkv: float32 [2048, 6144], P('fsdp')
- grad_w_beta: float32 [2048, 16], P('fsdp')
- grad_conv_weight: float32 [2048, 12], P('fsdp')
- grad_out_gain: float32 [128], replicated
- grad_w_out: float32 [2048, 2048], P('fsdp')
- grad_norm2_gain: float32 [2048], P('fsdp')
- grad_w_gate_up: float32 [2048, 11264], P('fsdp')
- grad_w_down: float32 [5632, 2048], P('fsdp')
All inputs are finite; a program needn't handle non-finite values.
Results may differ from a plain program's by a relative error of at most 0.023.
Values may be sent and summed in bfloat16 or wider, within the bound.
A program may use at most 448 MiB of HBM per device.

v0:
```python
import jax
import jax.numpy as jnp
from jax import lax
from jax.sharding import PartitionSpec as P

H = 16
DK = 128
SPAN = 64
EPS = 1e-06
HIGH = lax.Precision.HIGHEST


def from_behind(array, axis, by):
    devices = lax.axis_size(axis)
    pairs = [(i, i + by) for i in range(devices) if 0 <= i + by < devices]
    return lax.ppermute(array, axis, pairs)


def rms_scale(values, gain):
    return values * lax.rsqrt(jnp.mean(values * values, axis=-1, keepdims=True) + EPS) * gain


def conv_table(conv_full):
    width = conv_full.shape[0]
    tap_count = conv_full.shape[1] // 3
    return (
        conv_full.astype(jnp.float32)
        .reshape(width, 3, tap_count)
        .transpose(1, 0, 2)
        .reshape(3 * width, tap_count)
    )


def pre_mix(extended, table, beta_logits):
    tap_count = table.shape[1]
    length = extended.shape[1] - tap_count + 1
    sequences = extended.shape[0]
    width = extended.shape[2] // 3
    mixed = extended[:, 0:length, :] * table[:, 0]
    for tap_index in range(1, tap_count):
        mixed = mixed + extended[:, tap_index : tap_index + length, :] * table[:, tap_index]
    active = jax.nn.silu(mixed)
    query = active[:, :, :width].reshape(sequences, length, H, DK) * DK ** (-0.5)
    key = active[:, :, width : 2 * width].reshape(sequences, length, H, DK)
    key = key * lax.rsqrt(jnp.sum(key * key, axis=-1, keepdims=True) + EPS)
    value = active[:, :, 2 * width :].reshape(sequences, length, H, DK)
    return (query, key, value, jax.nn.sigmoid(beta_logits))


def delta_rule(query, key, value, beta):
    sequences, length, heads, depth = query.shape
    count = length // SPAN

    def blocks(array):
        return array.reshape(sequences, count, SPAN, heads, -1).transpose(1, 0, 3, 2, 4)

    q_blocks = blocks(query)
    k_blocks = blocks(key)
    v_blocks = blocks(value)
    b_blocks = blocks(beta[..., None])
    gram = jnp.einsum("nshcd,nshmd->nshcm", k_blocks, k_blocks, precision=HIGH)
    below = jnp.tril(jnp.ones((SPAN, SPAN), jnp.float32), -1)
    inclusive = jnp.tril(jnp.ones((SPAN, SPAN), jnp.float32))
    system = jnp.eye(SPAN, dtype=jnp.float32) + below * (b_blocks * gram)
    targets = jnp.concatenate([b_blocks * k_blocks, b_blocks * v_blocks], axis=-1)
    solved = lax.linalg.triangular_solve(
        system, targets, left_side=True, lower=True, unit_diagonal=True
    )
    wy_key = solved[..., :depth]
    wy_value = solved[..., depth:]
    within = inclusive * jnp.einsum("nshcd,nshmd->nshcm", q_blocks, k_blocks, precision=HIGH)

    def advance(state, pieces):
        key_part, value_part, query_part, key_raw, attend = pieces
        fresh = value_part - jnp.einsum("shcd,shde->shce", key_part, state, precision=HIGH)
        result = jnp.einsum("shcd,shde->shce", query_part, state, precision=HIGH)
        result = result + jnp.einsum("shcm,shme->shce", attend, fresh, precision=HIGH)
        state = state + jnp.einsum("shcd,shce->shde", key_raw, fresh, precision=HIGH)
        return (state, result)

    start = jnp.zeros((sequences, heads, depth, value.shape[-1]), jnp.float32)
    final, outputs = lax.scan(advance, start, (wy_key, wy_value, q_blocks, k_blocks, within))
    return outputs.transpose(1, 0, 3, 2, 4).reshape(sequences, length, heads, -1)


def row_term(left, right):

    def term(start, count):
        return lax.dot_general(
            left, right, (((0,), (0,)), ((), ())), preferred_element_type=jnp.float32
        )

    return term


def reduce_rows(term, total_rows):
    shards = lax.axis_size("fsdp")
    summed = lax.psum_scatter(
        term(jnp.int32(0), total_rows // shards * lax.axis_size("fsdp")).astype(jnp.bfloat16),
        "fsdp",
        scatter_dimension=0,
        tiled=True,
    )
    return lax.psum(summed, "seq").astype(jnp.float32)


def against(left, right):
    return lax.dot_general(
        left, right, (((1,), (1,)), ((), ())), preferred_element_type=jnp.float32
    )


def per_device(
    inputs,
    cotangent,
    norm1_gain,
    w_qkv,
    w_beta,
    conv_weight,
    out_gain,
    w_out,
    norm2_gain,
    w_gate_up,
    w_down,
):
    gathered = (
        lax.all_gather(norm1_gain, "fsdp", axis=0, tiled=True),
        lax.all_gather(w_qkv, "fsdp", axis=0, tiled=True),
        lax.all_gather(w_beta, "fsdp", axis=0, tiled=True),
        lax.all_gather(conv_weight, "fsdp", axis=0, tiled=True),
        lax.all_gather(w_out, "fsdp", axis=0, tiled=True),
        lax.all_gather(norm2_gain, "fsdp", axis=0, tiled=True),
        lax.all_gather(w_gate_up, "fsdp", axis=0, tiled=True),
    )
    gain_first, qkv_full, beta_full, conv_full, out_full, gain_second, gate_up_full = gathered
    down_full = lax.all_gather(w_down, "fsdp", axis=0, tiled=True)
    sequences, block, width = inputs.shape
    tokens = sequences * block
    hidden_width = down_full.shape[0]
    edge_rows = conv_full.shape[1] // 3 - 1
    residual = inputs.astype(jnp.float32).reshape(tokens, width)
    first_normed, first_back = jax.vjp(rms_scale, residual, gain_first.astype(jnp.float32))
    normed_first = first_normed.astype(jnp.bfloat16)
    projected = jnp.dot(normed_first, qkv_full, preferred_element_type=jnp.float32)
    projected = projected.astype(jnp.bfloat16).reshape(sequences, block, 3 * width)
    beta_logits = jnp.dot(normed_first, beta_full, preferred_element_type=jnp.float32).reshape(
        sequences, block, -1
    )
    before = from_behind(projected[:, block - edge_rows :, :], "seq", 1)
    extended = jnp.concatenate([before, projected], axis=1).astype(jnp.float32)
    table = conv_table(conv_full)
    mixer_inputs, mixer_back = jax.vjp(pre_mix, extended, table, beta_logits)
    sent_query = mixer_inputs[0].astype(jnp.bfloat16)
    sent_key = mixer_inputs[1].astype(jnp.bfloat16)
    sent_value = mixer_inputs[2].astype(jnp.bfloat16)
    sent_beta = mixer_inputs[3].astype(jnp.bfloat16)
    query, key, value, beta = (
        lax.all_to_all(sent_query, "seq", split_axis=2, concat_axis=1, tiled=True),
        lax.all_to_all(sent_key, "seq", split_axis=2, concat_axis=1, tiled=True),
        lax.all_to_all(sent_value, "seq", split_axis=2, concat_axis=1, tiled=True),
        lax.all_to_all(sent_beta, "seq", split_axis=2, concat_axis=1, tiled=True),
    )
    heads_out, delta_back = jax.vjp(
        delta_rule,
        query.astype(jnp.float32),
        key.astype(jnp.float32),
        value.astype(jnp.float32),
        beta.astype(jnp.float32),
    )
    returned = lax.all_to_all(
        heads_out.astype(jnp.bfloat16), "seq", split_axis=1, concat_axis=2, tiled=True
    )
    normed_heads, heads_back = jax.vjp(
        rms_scale, returned.astype(jnp.float32), out_gain.astype(jnp.float32)
    )
    attn_in = normed_heads.astype(jnp.bfloat16).reshape(tokens, width)
    middle = residual + jnp.dot(attn_in, out_full, preferred_element_type=jnp.float32)
    second_normed, second_back = jax.vjp(rms_scale, middle, gain_second.astype(jnp.float32))
    ffn_in = second_normed.astype(jnp.bfloat16)
    gate_up = jnp.dot(ffn_in, gate_up_full, preferred_element_type=jnp.float32)
    gate = gate_up[:, :hidden_width]
    upward = gate_up[:, hidden_width:]
    sigma = jax.nn.sigmoid(gate)
    hidden = (gate * sigma * upward).astype(jnp.bfloat16)
    result = middle + jnp.dot(hidden, down_full, preferred_element_type=jnp.float32)
    output = result.astype(jnp.bfloat16).reshape(sequences, block, width)
    upstream = cotangent.reshape(tokens, width)
    grad_down = reduce_rows(row_term(hidden, upstream), hidden_width)
    grad_hidden = against(upstream, down_full)
    grad_gate = grad_hidden * upward * sigma * (1.0 + gate * (1.0 - sigma))
    grad_up = grad_hidden * gate * sigma
    grad_gate_up = jnp.concatenate([grad_gate, grad_up], axis=1).astype(jnp.bfloat16)
    grad_w_gate_up = reduce_rows(row_term(ffn_in, grad_gate_up), width)
    grad_ffn_in = against(grad_gate_up, gate_up_full)
    grad_middle_norm, grad_gain_second = second_back(grad_ffn_in)
    grad_middle = upstream.astype(jnp.float32) + grad_middle_norm
    grad_branch = grad_middle.astype(jnp.bfloat16)
    grad_w_out = reduce_rows(row_term(attn_in, grad_branch), width)
    grad_attn_in = against(grad_branch, out_full).reshape(sequences, block, H, DK)
    grad_returned, grad_gain_heads = heads_back(grad_attn_in)
    grad_heads = lax.all_to_all(
        grad_returned.astype(jnp.bfloat16), "seq", split_axis=2, concat_axis=1, tiled=True
    )
    grad_query, grad_key, grad_value, grad_beta = delta_back(grad_heads.astype(jnp.float32))
    back_query, back_key, back_value, back_beta = (
        lax.all_to_all(
            grad_query.astype(jnp.bfloat16), "seq", split_axis=1, concat_axis=2, tiled=True
        ),
        lax.all_to_all(
            grad_key.astype(jnp.bfloat16), "seq", split_axis=1, concat_axis=2, tiled=True
        ),
        lax.all_to_all(
            grad_value.astype(jnp.bfloat16), "seq", split_axis=1, concat_axis=2, tiled=True
        ),
        lax.all_to_all(
            grad_beta.astype(jnp.bfloat16), "seq", split_axis=1, concat_axis=2, tiled=True
        ),
    )
    grad_extended, grad_table, grad_logits = mixer_back(
        (
            back_query.astype(jnp.float32),
            back_key.astype(jnp.float32),
            back_value.astype(jnp.float32),
            back_beta.astype(jnp.float32),
        )
    )
    after = from_behind(grad_extended[:, :edge_rows, :].astype(jnp.bfloat16), "seq", -1).astype(
        jnp.float32
    )
    grad_projected = grad_extended[:, edge_rows:, :]
    grad_projected = grad_projected.at[:, block - edge_rows :, :].add(after)
    grad_proj_low = grad_projected.astype(jnp.bfloat16).reshape(tokens, 3 * width)
    grad_logits_low = grad_logits.astype(jnp.bfloat16).reshape(tokens, -1)
    grad_w_qkv = reduce_rows(row_term(normed_first, grad_proj_low), width)
    grad_beta_full = lax.dot_general(
        normed_first, grad_logits_low, (((0,), (0,)), ((), ())), preferred_element_type=jnp.float32
    )
    grad_normed_first = against(grad_proj_low, qkv_full) + against(grad_logits_low, beta_full)
    grad_residual_norm, grad_gain_first = first_back(grad_normed_first)
    grad_input = (grad_middle + grad_residual_norm).reshape(sequences, block, width)
    grad_conv = grad_table.reshape(3, width, -1).transpose(1, 0, 2).reshape(width, -1)
    summed = lax.psum(
        (grad_gain_first, grad_beta_full, grad_conv, grad_gain_heads, grad_gain_second),
        ("fsdp", "seq"),
    )
    share = width // lax.axis_size("fsdp")
    offset = lax.axis_index("fsdp") * share

    def own_rows(array):
        return lax.dynamic_slice_in_dim(array, offset, share, 0)

    return (
        output,
        grad_input,
        own_rows(summed[0]),
        grad_w_qkv,
        own_rows(summed[1]),
        own_rows(summed[2]),
        summed[3],
        grad_w_out,
        own_rows(summed[4]),
        grad_w_gate_up,
        grad_down,
    )


def solution(mesh):
    in_specs = (
        P("fsdp", "seq", None),
        P("fsdp", "seq", None),
        P("fsdp"),
        P("fsdp", None),
        P("fsdp", None),
        P("fsdp", None),
        P(),
        P("fsdp", None),
        P("fsdp"),
        P("fsdp", None),
        P("fsdp", None),
    )
    out_specs = (
        P("fsdp", "seq", None),
        P("fsdp", "seq", None),
        P("fsdp"),
        P("fsdp", None),
        P("fsdp", None),
        P("fsdp", None),
        P(),
        P("fsdp", None),
        P("fsdp"),
        P("fsdp", None),
        P("fsdp", None),
    )
    return jax.shard_map(
        per_device, mesh=mesh, in_specs=in_specs, out_specs=out_specs, check_vma=False
    )
```

profile of v0, /device:TPU:0, one launch (start us, length us, event | category | flops | bytes accessed | tf_op | source)
XLA Modules:
  0.0 2502.2 jit_solution(38190960428922679)
XLA Ops:
  10.1 13.6 all-gather
  23.7 24.1 all_gather.27
  51.0 3.6 all-to-all-start.1
  54.7 25.3 %all_gather.26 = bf16[2048,12]{0,1:T(8,128)(2,1)S(1)} all-gather(bf16[256,12]{0,1:T(8,128)(2,1)S(1)} %copy-done.77), channel_id=1, replica_groups=mesh['fsdp'=8,'seq'=4] {'fsdp'}, dimensions={0}, use_global_device_ids=true | all-gather | bytes 55296 | tf_op jit(solution)/shard_map/all_gather | solution.py:130
  80.0 153.2 %all-gather.7.cloned.1.call-done = bf16[2048,6144]{1,0:T(8,128)(2,1)} async-done(((bf16[256,6144]{1,0:T(8,128)(2,1)}), bf16[2048,6144]{1,0:T(8,128)(2,1)}) %all-gather.7.cloned.1.call-update) | async-done | bytes 25165840 | tf_op jit(solution)/shard_map/all_gather | solution.py:128
  233.2 12.3 fusion.79
  251.5 5.4 fusion.82
  262.7 4.5 all-to-all-start
  268.5 12.8 all-to-all-done
  281.3 3.5 all-to-all-start.3
  287.6 11.2 all-to-all-done.3
  299.8 4.0 all-to-all-start.2
  306.9 10.2 all-to-all-done.2
  322.4 315.2 %custom-call.7 = f32[16,1,4,1,64,64]{4,5,3,2,1,0:T(8,128)S(1)} custom-call(f32[16,1,4,1,64,64]{5,4,3,2,1,0:T(8,128)} %add_bitcast_fusion), custom_call_target="InvertDiagBlocksLowerTriangular" | custom-call | tf_op jit(solution)/shard_map/jvp()/triangular_solve | solution.py:66
  637.7 4.7 multiply_bitcast_fusion.1
  645.5 3.8 fusion.83
  653.0 107.2 %while.43 = (s32[]{:T(128)}, f32[1,4,128,128]{3,2,1,0:T(8,128)S(1)}, bf16[16,1,4,64,128]{4,3,0,2,1:T(8,128)(2,1)}, f32[16,1,4,128,128]{4,3,2,1,0:T(8,128)}, f32[...) while((s32[]{:T(128)}, ...), condition=%wide.region_3.4_spmd.clone, body=%wide.region_2.3_spmd.clone.sunk | while | flops 176553984 | bytes 3148948 | solution.py:82
  760.2 3.8 copy.375
  764.0 4.3 all-to-all-start.4
  768.4 8.8 all-gather.1
  777.2 4.2 all-to-all-done.4
  796.5 6.5 multiply_reduce_fusion.8
  803.1 24.2 fusion.211
  827.3 83.8 %all-gather.13.cloned.1.call-done = bf16[5632,2048]{1,0:T(8,128)(2,1)} async-done(((bf16[704,2048]{1,0:T(8,128)(2,1)}), bf16[5632,2048]{1,0:T(8,128)(2,1)}) %all-gather.13.cloned.1.call-update) | async-done | bytes 23068688 | tf_op jit(solution)/shard_map/all_gather | solution.py:136
  911.2 18.7 multiply_convert_fusion.1
  929.9 22.1 multiply_reduce_fusion.4
  955.3 5.8 convolution_convert_fusion.4
  961.1 12.9 convolution_convert_fusion.1
  974.1 3.3 copy.381
  977.4 8.4 multiply_reduce_fusion.5
  985.8 3.8 reshape.1082
  994.0 4.0 fusion.165
  998.0 4.1 all-to-all-start.5
  1002.1 14.2 all-to-all-done.5
  1025.9 241.0 %while.44 = (s32[]{:T(128)}, f32[1,4,128,128]{2,3,1,0:T(8,128)S(1)}, f32[16,1,4,64,128]{4,3,2,1,0:T(8,128)}, f32[16,1,4,64,128]{4,3,2,1,0:T(8,128)}, f32[16,1,4,...) while((s32[]{:T(128)}, ...), condition=%wide.region_9.10_spmd.clone, body=%wide.region_8.9_spmd.clone.sunk | while | flops 352747520 | bytes 4728510 | solution.py:82
  1266.9 5.8 fusion.106
  1272.7 4.7 fusion.86
  1277.5 3.8 multiply_reduce_fusion.6
  1285.0 3.6 fusion.153
  1290.5 4.2 all-to-all-start.7
  1299.5 8.7 all-to-all-done.7
  1308.2 4.3 all-to-all-start.8
  1317.4 4.0 fusion.115
  1328.9 4.2 all-to-all-start.6
  1337.3 3.6 mul.664
  1355.8 5.9 add_add_fusion.1
  1361.8 10.6 multiply_reduce_fusion.3
  1372.4 6.3 broadcast_multiply_fusion
  1378.7 6.5 pad_add_fusion
  1387.5 3.5 slice.128
  1393.8 14.0 convolution_convert_fusion.2
  1409.4 21.2 convolution_convert_fusion
  1436.1 8.7 all_to_all.105
  1450.2 204.2 %reduce-scatter.7.cloned.1.call-done = bf16[256,6144]{1,0:T(8,128)(2,1)} async-done(((bf16[2048,6144]{1,0:T(8,128)(2,1)}), bf16[256,6144]{1,0:T(8,128)(2,1)}) %reduce-scatter.7.cloned.1.call-update) | async-done | bytes 3145744 | tf_op jit(solution)/shard_map/reduce_scatter | solution.py:98
  1654.4 444.5 %reduce-scatter.13.cloned.1.call-done = bf16[256,11264]{1,0:T(8,128)(2,1)} async-done(((bf16[2048,11264]{1,0:T(8,128)(2,1)}), bf16[256,11264]{1,0:T(8,128)(2,1)}) %reduce-scatter.13.cloned.1.call-update) | async-done | bytes 5767184
  2099.6 12.6 fusion.105
  2114.0 14.4 fusion.110
  2128.4 38.2 %all-reduce.14 = (f32[2048]{0:T(1024)S(1)}, f32[128]{0:T(128)}, f32[2048]{0:T(1024)S(1)}) all-reduce(f32[2048]{0:T(1024)S(1)} %get-tuple-element.617, f32[128]{0:T(128)S(1)} %bitcast_reduce_fusion, f32[2048]{0:T(1024)S(1)} %copy-done.78), channel_id=1, replica_groups=mesh['fsdp'=8,'seq'=4] {'fsdp','seq'}, use_global_device_ids=true, to_apply=%region_16.17 | all-reduce | flops 4224 | bytes 33792 | tf_op jit(solution)/shard_map/psum | solution.py:242
  2168.0 3.4 fusion.119
  2171.4 58.3 %all-reduce.20.cloned.1.call-done = (f32[2048,16]{0,1:T(8,128)}, f32[2048,12]{0,1:T(8,128)}) async-done(((f32[2048,16]{0,1:T(8,128)}, f32[2048,12]{0,1:T(8,128)}), (f32[2048,16]{0,1:T(8,128)}, f32[2048,12]{0,1:T(8,128)})) %all-reduce.20.cloned.1.call-update) | async-done | bytes 229392 | tf_op jit(solution)/shard_map/psum | solution.py:242
  2232.4 246.7 %all-reduce.22.cloned.1.call-done = (bf16[256,6144]{1,0:T(8,128)(2,1)}, bf16[256,2048]{1,0:T(8,128)(2,1)}, bf16[256,11264]{1,0:T(8,128)(2,1)}, bf16[704,2048]{1,0:T(8,128)(2,1)}) async-done(((bf16[256,6144]{1,0:T(8,128)(2,1)}, bf16[256,2048]{1,0:T(8,128)(2,1)}, bf16[256,11264]{1,0:T(8,128)(2,1)}, bf16[704,2048]{1,0:T(8,128)(2,1)}), (bf16[256,6144]{1,0:T(8,128)(2,1)}, bf16[256,2048]{1,0:T(8,128)(2,1)}, ...) | async-done | bytes 12845072 | tf_op jit(solution)/shard_map/psum | solution.py:104
  2479.0 5.5 convert_element_type.516
  2486.1 5.8 convert_element_type.520
  2491.9 3.3 convert_element_type.522
  (540 shorter events, 484.8 us)
Async XLA Ops:
  7.2 226.0 %all-gather.7.cloned.1.call-start = ((), (), s32[]{:S(2)}) async-start(), calls=%async_computation.14 | async-start | bytes 28311552 | tf_op jit(solution)/shard_map/all_gather | solution.py:128
  7.9 788.6 %all-gather.9.cloned.1.call-start = ((), (), s32[]{:S(2)}) async-start(), calls=%async_computation.15 | async-start | bytes 9437184 | tf_op jit(solution)/shard_map/all_gather | solution.py:131
  8.7 794.4 %all-gather.11.cloned.1.call-start = ((), (), s32[]{:S(2)}) async-start(), calls=%async_computation.16 | async-start | bytes 51904512 | tf_op jit(solution)/shard_map/all_gather | solution.py:133
  9.4 14.2 copy-start.76
  9.4 38.4 %copy-start.27 = (bf16[1,256,2048]{2,1,0:T(8,128)(2,1)S(1)}, bf16[1,256,2048]{2,1,0:T(8,128)(2,1)}, u32[]{:S(2)}) copy-start(bf16[1,256,2048]{2,1,0:T(8,128)(2,1)} %param.17) | copy-start | bytes 3145732
  9.4 901.7 %all-gather.13.cloned.1.call-start = ((), (), s32[]{:S(2)}) async-start(), calls=%async_computation.17 | async-start | bytes 25952256 | tf_op jit(solution)/shard_map/all_gather | solution.py:136
  10.1 44.6 %copy-start.77 = (bf16[256,12]{0,1:T(8,128)(2,1)S(1)}, bf16[256,12]{0,1:T(8,128)(2,1)}, u32[]{:S(2)}) copy-start(bf16[256,12]{0,1:T(8,128)(2,1)} %param.22) | copy-start | bytes 18436
  23.7 221.9 %copy-start.46 = (f32[8,1,256]{2,1,0:T(1,128)}, f32[8,1,256]{2,1,0:T(1,128)S(1)}, u32[]{:S(2)}) copy-start(f32[8,1,256]{2,1,0:T(1,128)S(1)} %convert_element_type.540) | copy-start | bytes 24580
  47.8 6.9 copy-start.48
  48.7 196.9 %copy-start.70 = (f32[256]{0:T(256)}, f32[256]{0:T(256)S(1)}, u32[]{:S(2)}) copy-start(f32[256]{0:T(256)S(1)} %fusion.204) | copy-start | bytes 3076
  51.0 211.7 %all-to-all-start.1 = ((bf16[4,2,512]{2,1,0:T(2,128)(2,1)}), bf16[4,2,512]{2,1,0:T(2,128)(2,1)S(1)}, u32[]{:S(2)}, u32[]{:S(2)}) async-start(bf16[4,2,512]{2,1,0:T(2,128)(2,1)} %reshape.1133), calls=%async_computation.1 | async-start | bytes 16384 | tf_op jit(solution)/shard_map/all_to_all | solution.py:161
  245.6 5.0 collective-permute-start
  262.7 18.6 all-to-all-start
  281.3 6.3 copy-start.38
  281.3 17.5 all-to-all-start.3
  298.8 5.8 copy-start.39
  299.8 17.3 all-to-all-start.2
  303.8 333.9 %copy-start.44 = (f32[64,64]{1,0:T(8,128)}, f32[64,64]{1,0:T(8,128)S(1)}, u32[]{:S(2)}) copy-start(f32[64,64]{1,0:T(8,128)S(1)} %fusion.200) | copy-start | bytes 49156
  637.7 7.9 copy-start.7
  760.2 8.2 copy-start.80
  760.2 8.2 copy-start.81
  764.0 17.3 all-to-all-start.4
  768.3 681.9 %reduce-scatter.9.cloned.1.call-start = ((), (), s32[]{:S(2)}) async-start(), calls=%async_computation.19 | async-start | bytes 9437184 | tf_op jit(solution)/shard_map/reduce_scatter | solution.py:98
  789.9 6.6 copy-start.19
  803.0 126.9 %copy-start.30 = (f32[256,2048]{1,0:T(8,128)}, f32[256,2048]{1,0:T(8,128)S(1)}, u32[]{:S(2)}) copy-start(f32[256,2048]{1,0:T(8,128)S(1)} %get-tuple-element.707) | copy-start | bytes 6291460
  955.2 22.1 copy-start.3
  961.1 489.1 %reduce-scatter.11.cloned.1.call-start = ((), (), s32[]{:S(2)}) async-start(), calls=%async_computation.20 | async-start | bytes 25952256 | tf_op jit(solution)/shard_map/reduce_scatter | solution.py:98
  998.0 18.3 all-to-all-start.5
  1025.9 241.0 %copy-start.8 = (f32[16,1,4,1,64,64]{4,5,3,2,1,0:T(8,128)S(1)}, f32[16,1,4,1,64,64]{4,5,3,2,1,0:T(8,128)}, u32[]{:S(2)}) copy-start(f32[16,1,4,1,64,64]{4,5,3,2,1,0:T(8,128)} %copy-done.7) | copy-start | bytes 3145732
  1266.9 5.8 copy-start.2
  1266.9 5.8 copy-start.9
  1266.9 5.8 copy-start.10
  1272.7 12.3 copy-start.6
  1290.5 17.7 all-to-all-start.7
  1297.7 14.7 copy-start.59
  1308.2 20.7 all-to-all-start.8
  1328.9 21.0 all-to-all-start.6
  1333.2 321.2 %reduce-scatter.7.cloned.1.call-start = ((), (), s32[]{:S(2)}) async-start(), calls=%async_computation.18 | async-start | bytes 28311552 | tf_op jit(solution)/shard_map/reduce_scatter | solution.py:98
  1349.9 11.9 slice-start
  1355.8 5.9 slice-start.1
  1361.8 10.7 copy-start.51
  1361.8 10.7 copy-start.53
  1361.8 10.6 copy-start.55
  1361.8 10.6 copy-start.57
  1386.2 7.6 copy-start.47
  1386.2 7.6 copy-start.71
  1386.2 6.0 collective-permute-start.1
  1393.8 14.0 copy-start.26
  1407.9 691.0 %reduce-scatter.13.cloned.1.call-start = ((), (), s32[]{:S(2)}) async-start(), calls=%async_computation.21 | async-start | bytes 51904512
  1430.7 16.8 copy-start.69
  1430.7 16.8 copy-start.28
  1430.7 799.0 %all-reduce.20.cloned.1.call-start = ((), (), s32[]{:S(2)}) async-start(), calls=%async_computation.22 | async-start | bytes 524288 | tf_op jit(solution)/shard_map/psum | solution.py:242
  1432.7 16.6 copy-start.64
  1432.7 16.6 copy-start.65
  1432.7 16.6 copy-start.66
  1432.7 16.6 copy-start.67
  1450.1 1028.9 %all-reduce.22.cloned.1.call-start = ((), (), s32[]{:S(2)}) async-start(), calls=%async_computation.23 | async-start | bytes 25690112 | tf_op jit(solution)/shard_map/psum | solution.py:104
  2099.6 12.6 copy-start.49
  2114.0 14.4 copy-start.78
  2114.0 53.9 %copy-start.75 = (f32[256]{0:T(256)S(1)}, f32[256]{0:T(256)}, u32[]{:S(2)}) copy-start(f32[256]{0:T(256)} %copy-done.74) | copy-start | bytes 3076
  2114.0 54.0 %copy-start.4 = (f32[256,2048]{1,0:T(8,128)S(1)}, f32[256,2048]{1,0:T(8,128)}, u32[]{:S(2)}) copy-start(f32[256,2048]{1,0:T(8,128)} %copy-done.3) | copy-start | bytes 6291460
  2479.0 7.1 slice-start.2
  2479.0 7.1 slice-start.3
  2486.1 5.8 copy-start.42
  (43 other events, 105.4 us)
Sparse Core Ops, SparseCore 0:
  9.7 223.4 all-gather.6
  234.8 80.2 all-gather.8
  316.8 391.8 all-gather.10
  710.1 200.9 all-gather.12
  961.2 87.8 reduce-scatter.8
  1051.2 225.7 reduce-scatter.10
  1408.0 246.3 reduce-scatter.6
  1656.8 442.0 reduce-scatter.12
  2106.1 123.5 all-reduce.19
  2234.0 244.9 all-reduce.21
where the time goes:
time: 2520 us; the launch traced here: 2500 us
  waiting for transfers between devices  1260 us (50%)
  matrix products  546 us (22%)
  other arithmetic  419 us (17%)
  blocking collectives  119 us (5%)
  local copies, waits for them, and re-layouts  103 us (4%)
  starting transfers between devices  41.7 us (2%)
    unnamed x11, waiting for transfers between devices  447 us
    another operation x5, other arithmetic, delta_rule(): lax.linalg.triangular_solve(system, targets, left_side=True, lower=True,...  318 us
    psum x1, waiting for transfers between devices, reduce_rows(): return lax.psum(summed, 'seq').astype(jnp.float32)  247 us
    reduce_scatter x3, waiting for transfers between devices, reduce_rows(): lax.psum_scatter(term(jnp.int32(0), total_rows // shards * lax.axis_size(...  204 us
    all_gather x1, waiting for transfers between devices, per_device(): lax.all_gather(w_qkv, 'fsdp', axis=0, tiled=True)  153 us
    dot_general x48, matrix products, advance(): result = jnp.einsum('shcd,shde->shce', query_part, state, precision=HIGH)  92.6 us
    dot_general x48, matrix products, advance(): jnp.einsum('shcd,shce->shde', key_raw, fresh, precision=HIGH)  90 us
    all_gather x1, waiting for transfers between devices, per_device(): down_full = lax.all_gather(w_down, 'fsdp', axis=0, tiled=True)  83.8 us
  transfers between devices with their start and end apart: 21, of which 14 were waited for; matrix products, arithmetic and copies ran while one was open for 39% of the time, Pallas kernels for 0%

commit v1 on v0

--- a/solution.py
+++ b/solution.py
@@ -240,8 +240,10 @@
     grad_input = (grad_middle + grad_residual_norm).reshape(sequences, block, width)
     grad_conv = grad_table.reshape(3, width, -1).transpose(1, 0, 2).reshape(width, -1)
     summed = lax.psum(
-        (grad_gain_first, grad_beta_full, grad_conv, grad_gain_heads, grad_gain_second),
-        ("fsdp", "seq"),
+        lax.psum(
+            (grad_gain_first, grad_beta_full, grad_conv, grad_gain_heads, grad_gain_second), "seq"
+        ),
+        "fsdp",
     )
     share = width // lax.axis_size("fsdp")
     offset = lax.axis_index("fsdp") * share

time: 2520 us -> 2760 us (1.095)
  waiting for transfers between devices: 1260 us -> 1490 us
    reduce_scatter x3, waiting for transfers between devices: 204 us -> 529 us  [reduce_rows(): lax.psum_scatter(term(jnp.int32(0), total_rows // shards * lax.axis_size(...]
    psum x1, waiting for transfers between devices: 58.3 us -> 0.02 us  [per_device(): lax.psum((grad_gain_first, grad_beta_full, grad_conv, grad_gain_heads, gr...]
    unnamed x11 -> x12, waiting for transfers between devices: 447 us -> 448 us
  transfers between devices with their start and end apart: 21 -> 23, of which waited for: 14 -> 16; matrix products, arithmetic and copies ran while one was open for 39% -> 25% of each run, Pallas kernels for 0% -> 0%
where the time goes in v1:
time: 2760 us; the launch traced here: 2750 us
  waiting for transfers between devices  1490 us (54%)
  matrix products  563 us (20%)
  other arithmetic  415 us (15%)
  blocking collectives  115 us (4%)
  local copies, waits for them, and re-layouts  101 us (4%)
  starting transfers between devices  44.8 us (2%)
    reduce_scatter x3, waiting for transfers between devices, reduce_rows(): lax.psum_scatter(term(jnp.int32(0), total_rows // shards * lax.axis_size(...  529 us
    unnamed x12, waiting for transfers between devices  448 us
    another operation x5, other arithmetic, delta_rule(): lax.linalg.triangular_solve(system, targets, left_side=True, lower=True,...  318 us
    psum x1, waiting for transfers between devices, reduce_rows(): return lax.psum(summed, 'seq').astype(jnp.float32)  225 us
    all_gather x1, waiting for transfers between devices, per_device(): lax.all_gather(w_qkv, 'fsdp', axis=0, tiled=True)  153 us
    dot_general x48, matrix products, advance(): result = jnp.einsum('shcd,shde->shce', query_part, state, precision=HIGH)  92.2 us
    dot_general x48, matrix products, advance(): jnp.einsum('shcd,shde->shce', key_part, state, precision=HIGH)  91.3 us
    dot_general x48, matrix products, advance(): jnp.einsum('shcd,shce->shde', key_raw, fresh, precision=HIGH)  89.7 us
  transfers between devices with their start and end apart: 23, of which 16 were waited for; matrix products, arithmetic and copies ran while one was open for 25% of the time, Pallas kernels for 0%

profile of v1, /device:TPU:0, one launch (start us, length us, event | category | flops | bytes accessed | tf_op | source)
XLA Modules:
  0.0 2745.0 jit_solution(9402675148322685214)
XLA Ops:
  10.1 13.6 all-gather
  23.7 24.1 all_gather.27
  51.0 3.6 all-to-all-start.1
  54.6 25.3 all_gather.26
  80.0 153.2 %all-gather.7.cloned.1.call-done = bf16[2048,6144]{1,0:T(8,128)(2,1)} async-done(((bf16[256,6144]{1,0:T(8,128)(2,1)}), bf16[2048,6144]{1,0:T(8,128)(2,1)}) %all-gather.7.cloned.1.call-update) | async-done | bytes 25165840 | tf_op jit(solution)/shard_map/all_gather | solution.py:128
  233.2 12.3 fusion.79
  251.5 5.4 fusion.82
  262.4 4.5 all-to-all-start
  268.2 12.8 all-to-all-done
  281.0 3.5 all-to-all-start.3
  287.3 11.2 all-to-all-done.3
  299.5 3.7 all-to-all-start.2
  307.0 9.6 all-to-all-done.2
  321.9 315.2 %custom-call.7 = f32[16,1,4,1,64,64]{4,5,3,2,1,0:T(8,128)S(1)} custom-call(f32[16,1,4,1,64,64]{5,4,3,2,1,0:T(8,128)} %add_bitcast_fusion), custom_call_target="InvertDiagBlocksLowerTriangular" | custom-call | tf_op jit(solution)/shard_map/jvp()/triangular_solve | solution.py:66
  637.1 4.0 multiply_bitcast_fusion.1
  644.3 3.8 fusion.83
  652.9 117.3 %while.43 = (s32[]{:T(128)}, f32[1,4,128,128]{3,2,1,0:T(8,128)S(1)}, bf16[16,1,4,64,128]{4,3,0,2,1:T(8,128)(2,1)}, f32[16,1,4,128,128]{4,3,2,1,0:T(8,128)}, f32[...) while((s32[]{:T(128)}, ...), condition=%wide.region_3.4_spmd.clone, body=%wide.region_2.3_spmd.clone.sunk | while | flops 176553984 | bytes 3148948 | solution.py:82
  773.4 4.2 all-to-all-start.4
  777.6 9.3 all-gather.1
  787.0 3.8 all-to-all-done.4
  797.4 3.5 reshape.1092
  806.7 7.8 multiply_reduce_fusion.8
  814.5 24.8 fusion.211
  839.3 71.8 %all-gather.13.cloned.1.call-done = bf16[5632,2048]{1,0:T(8,128)(2,1)} async-done(((bf16[704,2048]{1,0:T(8,128)(2,1)}), bf16[5632,2048]{1,0:T(8,128)(2,1)}) %all-gather.13.cloned.1.call-update) | async-done | bytes 23068688 | tf_op jit(solution)/shard_map/all_gather | solution.py:136
  911.2 18.7 multiply_convert_fusion.1
  929.9 22.4 multiply_reduce_fusion.4
  956.1 9.0 multiply_reduce_fusion.5
  965.2 3.7 reshape.1082
  968.8 3.5 copy.469
  973.4 3.6 fusion.165
  977.0 4.2 all-to-all-start.5
  981.3 14.4 all-to-all-done.5
  1006.7 240.2 %while.44 = (s32[]{:T(128)}, f32[1,4,128,128]{2,3,1,0:T(8,128)S(1)}, f32[16,1,4,64,128]{4,3,2,1,0:T(8,128)}, f32[16,1,4,64,128]{4,3,2,1,0:T(8,128)}, f32[16,1,4,...) while((s32[]{:T(128)}, ...), condition=%wide.region_9.10_spmd.clone, body=%wide.region_8.9_spmd.clone.sunk | while | flops 352747520 | bytes 4728510 | solution.py:82
  1246.9 8.2 fusion.86
  1255.1 3.9 fusion.106
  1259.0 5.0 multiply_reduce_fusion.6
  1270.1 3.2 all-to-all-start.9
  1278.5 4.7 fusion.153
  1285.1 4.3 all-to-all-start.7
  1302.9 3.7 all-to-all-start.8
  1313.6 6.2 all-to-all-done.8
  1319.7 4.2 all-to-all-start.6
  1345.0 5.9 add_add_fusion.1
  1350.9 10.0 multiply_reduce_fusion.3
  1362.2 7.7 convolution_convert_fusion.4
  1371.7 12.1 convolution_convert_fusion.1
  1384.6 6.3 broadcast_multiply_fusion
  1390.9 6.5 pad_add_fusion
  1399.7 3.5 slice.128
  1405.8 14.4 convolution_convert_fusion.2
  1421.8 21.3 convolution_convert_fusion
  1443.8 52.3 %reduce-scatter.9.cloned.1.call-done = bf16[256,2048]{1,0:T(8,128)(2,1)} async-done(((bf16[2048,2048]{1,0:T(8,128)(2,1)}), bf16[256,2048]{1,0:T(8,128)(2,1)}) %reduce-scatter.9.cloned.1.call-update) | async-done | bytes 1048592 | tf_op jit(solution)/shard_map/reduce_scatter | solution.py:98
  1496.1 228.3 %reduce-scatter.11.cloned.1.call-done = bf16[704,2048]{1,0:T(8,128)(2,1)} async-done(((bf16[5632,2048]{1,0:T(8,128)(2,1)}), bf16[704,2048]{1,0:T(8,128)(2,1)}) %reduce-scatter.11.cloned.1.call-update) | async-done | bytes 2883600 | tf_op jit(solution)/shard_map/reduce_scatter | solution.py:98
  1724.4 248.0 %reduce-scatter.7.cloned.1.call-done = bf16[256,6144]{1,0:T(8,128)(2,1)} async-done(((bf16[2048,6144]{1,0:T(8,128)(2,1)}), bf16[256,6144]{1,0:T(8,128)(2,1)}) %reduce-scatter.7.cloned.1.call-update) | async-done | bytes 3145744 | tf_op jit(solution)/shard_map/reduce_scatter | solution.py:98
  1972.4 444.6 %reduce-scatter.13.cloned.1.call-done = bf16[256,11264]{1,0:T(8,128)(2,1)} async-done(((bf16[2048,11264]{1,0:T(8,128)(2,1)}), bf16[256,11264]{1,0:T(8,128)(2,1)}) %reduce-scatter.13.cloned.1.call-update) | async-done | bytes 5767184
  2417.8 12.4 fusion.105
  2431.9 14.5 fusion.110
  2446.4 16.1 all-reduce.16
  2462.5 26.7 all-reduce.14
  2490.5 3.5 fusion.119
  2496.7 225.4 %all-reduce.27.cloned.1.call-done = (bf16[256,6144]{1,0:T(8,128)(2,1)}, bf16[256,2048]{1,0:T(8,128)(2,1)}, bf16[256,11264]{1,0:T(8,128)(2,1)}, bf16[704,2048]{1,0:T(8,128)(2,1)}) async-done(((bf16[256,6144]{1,0:T(8,128)(2,1)}, bf16[256,2048]{1,0:T(8,128)(2,1)}, bf16[256,11264]{1,0:T(8,128)(2,1)}, bf16[704,2048]{1,0:T(8,128)(2,1)}), (bf16[256,6144]{1,0:T(8,128)(2,1)}, bf16[256,2048]{1,0:T(8,128)(2,1)}, ...) | async-done | bytes 12845072 | tf_op jit(solution)/shard_map/psum | solution.py:104
  2722.1 5.5 convert_element_type.516
  2729.2 5.8 convert_element_type.520
  2735.0 3.3 convert_element_type.522
  (517 shorter events, 500.2 us)
Async XLA Ops:
  7.2 226.0 %all-gather.7.cloned.1.call-start = ((), (), s32[]{:S(2)}) async-start(), calls=%async_computation.14 | async-start | bytes 28311552 | tf_op jit(solution)/shard_map/all_gather | solution.py:128
  7.9 798.8 %all-gather.9.cloned.1.call-start = ((), (), s32[]{:S(2)}) async-start(), calls=%async_computation.15 | async-start | bytes 9437184 | tf_op jit(solution)/shard_map/all_gather | solution.py:131
  8.7 805.8 %all-gather.11.cloned.1.call-start = ((), (), s32[]{:S(2)}) async-start(), calls=%async_computation.16 | async-start | bytes 51904512 | tf_op jit(solution)/shard_map/all_gather | solution.py:133
  9.4 14.2 copy-start.62
  9.4 38.4 %copy-start.24 = (bf16[1,256,2048]{2,1,0:T(8,128)(2,1)S(1)}, bf16[1,256,2048]{2,1,0:T(8,128)(2,1)}, u32[]{:S(2)}) copy-start(bf16[1,256,2048]{2,1,0:T(8,128)(2,1)} %param.17) | copy-start | bytes 3145732
  9.4 901.7 %all-gather.13.cloned.1.call-start = ((), (), s32[]{:S(2)}) async-start(), calls=%async_computation.17 | async-start | bytes 25952256 | tf_op jit(solution)/shard_map/all_gather | solution.py:136
  10.1 44.6 %copy-start.63 = (bf16[256,12]{0,1:T(8,128)(2,1)S(1)}, bf16[256,12]{0,1:T(8,128)(2,1)}, u32[]{:S(2)}) copy-start(bf16[256,12]{0,1:T(8,128)(2,1)} %param.22) | copy-start | bytes 18436
  23.7 221.9 %copy-start.39 = (f32[8,1,256]{2,1,0:T(1,128)}, f32[8,1,256]{2,1,0:T(1,128)S(1)}, u32[]{:S(2)}) copy-start(f32[8,1,256]{2,1,0:T(1,128)S(1)} %convert_element_type.540) | copy-start | bytes 24580
  47.8 6.8 copy-start.41
  48.7 196.9 %copy-start.57 = (f32[256]{0:T(256)}, f32[256]{0:T(256)S(1)}, u32[]{:S(2)}) copy-start(f32[256]{0:T(256)S(1)} %fusion.204) | copy-start | bytes 3076
  49.1 5.5 copy-start.55
  51.0 211.4 %all-to-all-start.1 = ((bf16[4,2,512]{2,1,0:T(2,128)(2,1)}), bf16[4,2,512]{2,1,0:T(2,128)(2,1)S(1)}, u32[]{:S(2)}, u32[]{:S(2)}) async-start(bf16[4,2,512]{2,1,0:T(2,128)(2,1)} %reshape.1133), calls=%async_computation.1 | async-start | bytes 16384 | tf_op jit(solution)/shard_map/all_to_all | solution.py:161
  245.6 4.9 collective-permute-start
  251.5 5.4 copy-start
  262.4 18.6 all-to-all-start
  281.0 6.3 copy-start.32
  281.0 17.6 all-to-all-start.3
  298.6 6.1 copy-start.33
  299.5 17.0 all-to-all-start.2
  637.1 4.0 copy-start.21
  648.1 3.3 copy-start.1
  770.3 7.4 copy-start.66
  770.3 7.4 copy-start.67
  773.4 17.4 all-to-all-start.4
  952.3 3.3 copy-start.18
  952.3 3.8 copy-start.20
  956.1 9.1 copy-start.2
  968.8 3.5 copy-start.27
  968.8 3.5 copy-start.30
  977.0 18.6 all-to-all-start.5
  1246.9 8.2 copy-start.7
  1246.9 8.2 copy-start.8
  1255.1 3.9 copy-start.10
  1259.0 5.0 copy-start.5
  1259.0 5.0 copy-start.13
  1270.1 15.0 all-to-all-start.9
  1273.4 4.8 copy-start.14
  1285.1 17.8 all-to-all-start.7
  1300.7 6.0 copy-start.56
  1300.7 6.0 copy-start.25
  1300.7 6.0 copy-start.40
  1300.8 6.0 copy-start.58
  1302.9 16.8 all-to-all-start.8
  1319.7 19.3 all-to-all-start.6
  1324.0 119.3 %all-reduce.25.cloned.1.call-start = ((), (), s32[]{:S(2)}) async-start(), calls=%async_computation.23 | async-start | bytes 524288 | tf_op jit(solution)/shard_map/psum | solution.py:243
  1326.9 3.2 copy-start.16
  1339.0 11.8 slice-start
  1345.0 5.9 slice-start.1
  1361.7 134.4 %reduce-scatter.9.cloned.1.call-start = ((), (), s32[]{:S(2)}) async-start(), calls=%async_computation.19 | async-start | bytes 9437184 | tf_op jit(solution)/shard_map/reduce_scatter | solution.py:98
  1369.9 354.5 %reduce-scatter.11.cloned.1.call-start = ((), (), s32[]{:S(2)}) async-start(), calls=%async_computation.20 | async-start | bytes 25952256 | tf_op jit(solution)/shard_map/reduce_scatter | solution.py:98
  1383.9 588.6 %reduce-scatter.7.cloned.1.call-start = ((), (), s32[]{:S(2)}) async-start(), calls=%async_computation.18 | async-start | bytes 28311552 | tf_op jit(solution)/shard_map/reduce_scatter | solution.py:98
  1398.4 6.0 collective-permute-start.1
  1405.8 14.4 copy-start.23
  1420.3 996.8 %reduce-scatter.13.cloned.1.call-start = ((), (), s32[]{:S(2)}) async-start(), calls=%async_computation.21 | async-start | bytes 51904512
  1443.2 1050.8 %all-reduce.23.cloned.1.call-start = ((), (), s32[]{:S(2)}) async-start(), calls=%async_computation.22 | async-start | bytes 524288 | tf_op jit(solution)/shard_map/psum | solution.py:242
  1443.8 1278.3 %all-reduce.27.cloned.1.call-start = ((), (), s32[]{:S(2)}) async-start(), calls=%async_computation.24 | async-start | bytes 25690112 | tf_op jit(solution)/shard_map/psum | solution.py:104
  2417.8 12.4 copy-start.42
  2431.9 14.5 copy-start.64
  2431.9 58.6 %copy-start.61 = (f32[256]{0:T(256)S(1)}, f32[256]{0:T(256)}, u32[]{:S(2)}) copy-start(f32[256]{0:T(256)} %copy-done.60) | copy-start | bytes 3076
  2431.9 58.6 %copy-start.3 = (f32[256,2048]{1,0:T(8,128)S(1)}, f32[256,2048]{1,0:T(8,128)}, u32[]{:S(2)}) copy-start(f32[256,2048]{1,0:T(8,128)} %copy-done.2) | copy-start | bytes 6291460
  2722.1 7.1 slice-start.2
  2722.1 5.5 copy-start.38
  2722.1 7.1 slice-start.3
  2729.2 5.8 copy-start.37
  (31 other events, 54.6 us)
Sparse Core Ops, SparseCore 0:
  9.7 223.4 all-gather.6
  234.8 80.2 all-gather.8
  316.8 391.8 all-gather.10
  710.1 201.0 all-gather.12
  1361.8 41.7 all-reduce.24
  1406.4 89.6 reduce-scatter.8
  1498.6 225.7 reduce-scatter.10
  1726.9 245.5 reduce-scatter.6
  1974.9 442.0 reduce-scatter.12
  2419.2 53.4 all-reduce.22
  2477.2 244.8 all-reduce.26
